TPU v7x, 256 devices: a whole 4x4x8 slice. The times are simulated.
256 devices in a mesh: ctx: 32 (over z, x_lo, core), head: 8 (over x_hi, y).
Axes of the slice: x: 4 (x_hi: 2, x_lo: 2; x = x_hi * 2 + x_lo), y: 4, z: 8, core: 2. Of those that a mesh axis runs over, the one named last changes fastest.
Arguments:
- block_order: int32 [64], replicated, may hold values from 0 to 63, as said below
- queries: bfloat16 [12288, 4096], P('ctx', 'head'), may hold values from -12 to 12
- key_head_matrix: bfloat16 [12288, 1024], P('ctx', 'head'), may hold values from -6 to 6
- value_head_matrix: bfloat16 [12288, 1024], P('ctx', 'head'), may hold values from -6 to 6
- out_weight: bfloat16 [4096, 4096], P('head'), may hold values from -0.125 to 0.125
- filter_taps: float32 [128, 4096], P(None, 'head'), may hold values from -0.5 to 0.5
- skip_gain: float32 [4096], P('head'), may hold values from 0.5 to 1.5
- gate_values: bfloat16 [12288, 4096], P('ctx', 'head'), may hold values from -4 to 4
Outputs:
- mixed_out: bfloat16 [12288, 4096], P('ctx', 'head')
Inputs may be any that keep to these rules, and one draw needn't show every extreme that they name: A permutation of the 64 sequence blocks; for every d, block_order[2 d] < 32 and block_order[2 d] + block_order[2 d + 1] = 63.
All inputs are finite; a program needn't handle non-finite values.
Results may differ from a plain program's by a relative error of at most 0.015.
Values may be sent and summed in bfloat16 or wider, within the bound.
No kernel may reach another device: no remote copies, remote signals or barrier semaphores. Data moves between devices by JAX's collectives and lax.ppermute only.
A program may use at most 64 MiB of HBM per device.

v0:
```python
import math
import jax
import jax.numpy as jnp
from jax import lax
from jax.sharding import PartitionSpec as P

HEAD_WIDTH = 128
QUERY_PER_KV = 4


def side_by_side(arrays, axis, dim, along):
    widths = [a.shape[along] for a in arrays]
    both = jnp.concatenate(arrays, axis=along)
    out = lax.all_gather(both, axis, axis=dim, tiled=True)
    return tuple(jnp.split(out, [sum(widths[:k]) for k in range(1, len(widths))], axis=along))


def in_blocks(x, dim, size):
    shape = x.shape
    tiles = x.reshape(*shape[:dim], size, shape[dim] // size, *shape[dim + 1 :])
    return jnp.moveaxis(tiles, dim, 0)


def sum_at_owner(x, axis, dim):
    size = lax.axis_size(axis)
    tiles = lax.all_to_all(in_blocks(x, dim, size), axis, 0, 0, tiled=True)
    return jnp.sum(tiles.astype(jnp.float32), axis=0)


def lookup(table_values, index_values):
    matches = jnp.arange(table_values.shape[0], dtype=jnp.int32)[None, :] == index_values[:, None]
    return jnp.sum(jnp.where(matches, table_values[None, :], 0), axis=1)


def shards(
    block_order,
    queries,
    key_head_matrix,
    value_head_matrix,
    out_weight,
    filter_taps,
    skip_gain,
    gate_values,
):
    local_rows = queries.shape[0]
    block_rows = local_rows // 2
    shared_heads = key_head_matrix.shape[1] // HEAD_WIDTH
    position = lax.axis_index("ctx")
    own_blocks = 2 * position + jnp.arange(2, dtype=jnp.int32)
    own_order = lookup(block_order, own_blocks)
    query_place = (
        own_order[:, None] * block_rows + jnp.arange(block_rows, dtype=jnp.int32)[None, :]
    ).reshape(local_rows)
    query_heads = queries.reshape(local_rows, shared_heads, QUERY_PER_KV, HEAD_WIDTH)
    scaling = 1.0 / math.sqrt(HEAD_WIDTH)

    def attend_block(state_now, key_block, value_block, offset):
        running, row_total, summed = state_now
        key_count = key_block.shape[0]
        key_index = offset + jnp.arange(key_count, dtype=jnp.int32)
        key_place = (
            lookup(block_order, key_index // block_rows) * block_rows + key_index % block_rows
        )
        allowed = key_place[None, :] <= query_place[:, None]
        scores = (
            jnp.einsum("qhgd,khd->hgqk", query_heads, key_block, preferred_element_type=jnp.float32)
            * scaling
        )
        scores = jnp.where(allowed, scores, -1e30)
        newest = jnp.maximum(running, jnp.max(scores, axis=-1))
        weight = jnp.where(allowed, jnp.exp(scores - newest[..., None]), 0.0)
        factor = jnp.exp(running - newest)
        row_total = row_total * factor + jnp.sum(weight, axis=-1)
        summed = summed * factor[..., None] + jnp.einsum(
            "hgqk,khd->hgqd",
            weight.astype(jnp.bfloat16),
            value_block,
            preferred_element_type=jnp.float32,
        )
        return (newest, row_total, summed)

    start_state = (
        jnp.full((shared_heads, QUERY_PER_KV, local_rows), -1e30, jnp.float32),
        jnp.zeros((shared_heads, QUERY_PER_KV, local_rows), jnp.float32),
        jnp.zeros((shared_heads, QUERY_PER_KV, local_rows, HEAD_WIDTH), jnp.float32),
    )
    key_piece, value_piece = side_by_side((key_head_matrix, value_head_matrix), "ctx", 0, 1)
    key_count = key_piece.shape[0]
    sub_rows = math.gcd(key_count, 1024)
    steps_count = key_count // sub_rows
    key_split = key_piece.reshape(steps_count, sub_rows, shared_heads, HEAD_WIDTH)
    value_split = value_piece.reshape(steps_count, sub_rows, shared_heads, HEAD_WIDTH)

    def one_step(carried, operands):
        key_block, value_block, block_number = operands
        return (attend_block(carried, key_block, value_block, block_number * sub_rows), None)

    result, unused = lax.scan(
        one_step, start_state, (key_split, value_split, jnp.arange(steps_count, dtype=jnp.int32))
    )
    running, row_total, summed = result
    attended = (
        jnp.transpose(summed / row_total[..., None], (2, 0, 1, 3))
        .reshape(local_rows, -1)
        .astype(jnp.bfloat16)
    )
    partials = jnp.dot(attended, out_weight, preferred_element_type=jnp.float32)
    projected = sum_at_owner(partials.astype(jnp.bfloat16), "head", 1).astype(jnp.bfloat16)
    channels = projected.shape[1]
    reach_rows = filter_taps.shape[0] - 1
    blocks_here = projected.reshape(2, block_rows, channels)
    tail_rows = blocks_here[:, block_rows - reach_rows :, :]
    wanted = own_order - 1
    piece = lax.all_gather(tail_rows, "ctx", axis=0, tiled=True)
    piece_count = piece.shape[0]
    held_blocks = lookup(block_order, jnp.arange(piece_count, dtype=jnp.int32))
    matches = (held_blocks[None, :] == wanted[:, None]).astype(jnp.bfloat16)
    halo_rows = jnp.einsum(
        "sn,nrc->src", matches, piece, preferred_element_type=jnp.float32
    ).astype(jnp.bfloat16)
    extended = jnp.concatenate([halo_rows, blocks_here], axis=1).astype(jnp.float32)
    reversed_taps = jnp.flip(filter_taps, 0)
    kernel = reversed_taps[:, None, :]
    filtered = lax.conv_general_dilated(
        extended,
        kernel,
        (1,),
        "VALID",
        dimension_numbers=("NHC", "HIO", "NHC"),
        feature_group_count=channels,
        precision=lax.Precision.HIGHEST,
    )
    gate_here = gate_values.reshape(2, block_rows, channels).astype(jnp.float32)
    mixed_rows = gate_here * (filtered + skip_gain[None, None, :] * blocks_here.astype(jnp.float32))
    return mixed_rows.reshape(local_rows, channels).astype(jnp.bfloat16)


def solution(mesh):
    return jax.shard_map(
        shards,
        mesh=mesh,
        in_specs=(
            P(),
            P("ctx", "head"),
            P("ctx", "head"),
            P("ctx", "head"),
            P("head", None),
            P(None, "head"),
            P("head"),
            P("ctx", "head"),
        ),
        out_specs=P("ctx", "head"),
        check_vma=False,
    )
```

profile of v0, /device:TPU:1, one launch (start us, length us, event | category | flops | bytes accessed | tf_op | source)
XLA Modules:
  0.0 391.9 jit_solution(11266941806770182200)
XLA Ops:
  6.5 1.6 pad_maximum_fusion
  8.3 1.2 copy.44
  9.8 0.8 fusion.46
  10.6 71.8 %all-gather.3.cloned.1.call-done = bf16[12288,256]{1,0:T(8,128)(2,1)} async-done(((bf16[384,256]{1,0:T(8,128)(2,1)}), bf16[12288,256]{1,0:T(8,128)(2,1)}) %all-gather.3.cloned.1.call-update) | async-done | bytes 6291472 | tf_op jit(solution)/shard_map/all_gather | solution.py:14
  82.5 4.7 %fusion.50 = (bf16[12288,128]{1,0:T(8,128)(2,1)}, bf16[12288,128]{1,0:T(8,128)(2,1)}) fusion(bf16[12288,256]{1,0:T(8,128)(2,1)} %all-gather.3.cloned.1.call-done), kind=kLoop, calls=%fused_computation.69 | loop fusion | bytes 12582912 | tf_op jit(solution)/shard_map/split | solution.py:15
  87.2 156.6 %while.17 = (s32[]{:T(128)}, f32[1,4,384]{2,1,0:T(4,128)S(1)}, f32[1,4,384]{2,1,0:T(4,128)S(1)}, f32[1,4,384,128]{3,2,1,0:T(8,128)S(1)}, s32[12]{0:T(128)S(1)}, ...) while((s32[]{:T(128)}, f32[1,4,384]{2,1,0:T(4,128)S(1)}, ...), condition=%wide.region_6.7_spmd.clone, body=%wide.region_2.6_spmd.clone.sunk | while | flops 826960256 | bytes 48233928 | solution.py:98
  87.2 0.6 dynamic_slice.38
  89.0 4.8 %fusion.66 = (f32[4,384]{1,0:T(4,128)S(1)}, f32[1024,384,4]{1,0,2:T(8,128)}) fusion(pred[384,1024]{0,1:T(8,128)(4,1)S(1)} %broadcast_compare_fusion.2, bf16[384,1,4,128]{3,0,2,1:T(8,128)(2,1)S(1)} %get-tuple-element.342, bf16[12,1024,1,128]{3,1,2,0:T(8,128)(2,1)} %get-tuple-element.341, s32[]{:T(128)} %get-tuple-element.322), kind=kOutput, calls=%fused_computation.3.clone.1 | convolution fusion | flops 407370240 | bytes 7346688 | tf_op jit(solution)/shard_map/while/body/eval_jaxpr/qhgd,khd->hgqk/dot_general | solution.py:66
  93.8 4.8 %fusion.69 = f32[1,4,384,128]{3,2,1,0:T(8,128)S(1)} fusion(f32[1024,384,4]{1,0,2:T(8,128)} %get-tuple-element.307, f32[4,384]{1,0:T(4,128)S(1)} %bitcast.111, pred[384,1024]{0,1:T(8,128)(4,1)S(1)} %broadcast_compare_fusion.2, f32[1,4,384,128]{3,2,1,0:T(8,128)S(1)} %get-tuple-element.325, f32[4,384]{1,0:T(4,128)S(1)} %get-tuple-element.308, ...), kind=kOutput, calls=%fused_computation.10.clone.1 | convolution fusion | flops 411107328 | bytes 8532481 | tf_op jit(solution)/shard_map/while/body/eval_jaxpr/hgqk,khd->hgqd/dot_general | solution.py:74
  98.7 1.6 fusion.68
  100.3 0.6 dynamic_slice.38
  102.1 4.8 %fusion.66 = (f32[4,384]{1,0:T(4,128)S(1)}, f32[1024,384,4]{1,0,2:T(8,128)}) fusion(pred[384,1024]{0,1:T(8,128)(4,1)S(1)} %broadcast_compare_fusion.2, bf16[384,1,4,128]{3,0,2,1:T(8,128)(2,1)S(1)} %get-tuple-element.342, bf16[12,1024,1,128]{3,1,2,0:T(8,128)(2,1)} %get-tuple-element.341, s32[]{:T(128)} %get-tuple-element.322), kind=kOutput, calls=%fused_computation.3.clone.1 | convolution fusion | flops 407370240 | bytes 7346688 | tf_op jit(solution)/shard_map/while/body/eval_jaxpr/qhgd,khd->hgqk/dot_general | solution.py:66
  106.9 4.8 %fusion.69 = f32[1,4,384,128]{3,2,1,0:T(8,128)S(1)} fusion(f32[1024,384,4]{1,0,2:T(8,128)} %get-tuple-element.307, f32[4,384]{1,0:T(4,128)S(1)} %bitcast.111, pred[384,1024]{0,1:T(8,128)(4,1)S(1)} %broadcast_compare_fusion.2, f32[1,4,384,128]{3,2,1,0:T(8,128)S(1)} %get-tuple-element.325, f32[4,384]{1,0:T(4,128)S(1)} %get-tuple-element.308, ...), kind=kOutput, calls=%fused_computation.10.clone.1 | convolution fusion | flops 411107328 | bytes 8532481 | tf_op jit(solution)/shard_map/while/body/eval_jaxpr/hgqk,khd->hgqd/dot_general | solution.py:74
  111.7 1.6 fusion.68
  113.3 0.6 dynamic_slice.38
  115.2 4.8 %fusion.66 = (f32[4,384]{1,0:T(4,128)S(1)}, f32[1024,384,4]{1,0,2:T(8,128)}) fusion(pred[384,1024]{0,1:T(8,128)(4,1)S(1)} %broadcast_compare_fusion.2, bf16[384,1,4,128]{3,0,2,1:T(8,128)(2,1)S(1)} %get-tuple-element.342, bf16[12,1024,1,128]{3,1,2,0:T(8,128)(2,1)} %get-tuple-element.341, s32[]{:T(128)} %get-tuple-element.322), kind=kOutput, calls=%fused_computation.3.clone.1 | convolution fusion | flops 407370240 | bytes 7346688 | tf_op jit(solution)/shard_map/while/body/eval_jaxpr/qhgd,khd->hgqk/dot_general | solution.py:66
  120.0 4.8 %fusion.69 = f32[1,4,384,128]{3,2,1,0:T(8,128)S(1)} fusion(f32[1024,384,4]{1,0,2:T(8,128)} %get-tuple-element.307, f32[4,384]{1,0:T(4,128)S(1)} %bitcast.111, pred[384,1024]{0,1:T(8,128)(4,1)S(1)} %broadcast_compare_fusion.2, f32[1,4,384,128]{3,2,1,0:T(8,128)S(1)} %get-tuple-element.325, f32[4,384]{1,0:T(4,128)S(1)} %get-tuple-element.308, ...), kind=kOutput, calls=%fused_computation.10.clone.1 | convolution fusion | flops 411107328 | bytes 8532481 | tf_op jit(solution)/shard_map/while/body/eval_jaxpr/hgqk,khd->hgqd/dot_general | solution.py:74
  124.8 1.6 fusion.68
  126.4 0.6 dynamic_slice.38
  128.2 4.8 %fusion.66 = (f32[4,384]{1,0:T(4,128)S(1)}, f32[1024,384,4]{1,0,2:T(8,128)}) fusion(pred[384,1024]{0,1:T(8,128)(4,1)S(1)} %broadcast_compare_fusion.2, bf16[384,1,4,128]{3,0,2,1:T(8,128)(2,1)S(1)} %get-tuple-element.342, bf16[12,1024,1,128]{3,1,2,0:T(8,128)(2,1)} %get-tuple-element.341, s32[]{:T(128)} %get-tuple-element.322), kind=kOutput, calls=%fused_computation.3.clone.1 | convolution fusion | flops 407370240 | bytes 7346688 | tf_op jit(solution)/shard_map/while/body/eval_jaxpr/qhgd,khd->hgqk/dot_general | solution.py:66
  133.0 4.8 %fusion.69 = f32[1,4,384,128]{3,2,1,0:T(8,128)S(1)} fusion(f32[1024,384,4]{1,0,2:T(8,128)} %get-tuple-element.307, f32[4,384]{1,0:T(4,128)S(1)} %bitcast.111, pred[384,1024]{0,1:T(8,128)(4,1)S(1)} %broadcast_compare_fusion.2, f32[1,4,384,128]{3,2,1,0:T(8,128)S(1)} %get-tuple-element.325, f32[4,384]{1,0:T(4,128)S(1)} %get-tuple-element.308, ...), kind=kOutput, calls=%fused_computation.10.clone.1 | convolution fusion | flops 411107328 | bytes 8532481 | tf_op jit(solution)/shard_map/while/body/eval_jaxpr/hgqk,khd->hgqd/dot_general | solution.py:74
  137.8 1.6 fusion.68
  139.4 0.6 dynamic_slice.38
  141.3 4.8 %fusion.66 = (f32[4,384]{1,0:T(4,128)S(1)}, f32[1024,384,4]{1,0,2:T(8,128)}) fusion(pred[384,1024]{0,1:T(8,128)(4,1)S(1)} %broadcast_compare_fusion.2, bf16[384,1,4,128]{3,0,2,1:T(8,128)(2,1)S(1)} %get-tuple-element.342, bf16[12,1024,1,128]{3,1,2,0:T(8,128)(2,1)} %get-tuple-element.341, s32[]{:T(128)} %get-tuple-element.322), kind=kOutput, calls=%fused_computation.3.clone.1 | convolution fusion | flops 407370240 | bytes 7346688 | tf_op jit(solution)/shard_map/while/body/eval_jaxpr/qhgd,khd->hgqk/dot_general | solution.py:66
  146.1 4.8 %fusion.69 = f32[1,4,384,128]{3,2,1,0:T(8,128)S(1)} fusion(f32[1024,384,4]{1,0,2:T(8,128)} %get-tuple-element.307, f32[4,384]{1,0:T(4,128)S(1)} %bitcast.111, pred[384,1024]{0,1:T(8,128)(4,1)S(1)} %broadcast_compare_fusion.2, f32[1,4,384,128]{3,2,1,0:T(8,128)S(1)} %get-tuple-element.325, f32[4,384]{1,0:T(4,128)S(1)} %get-tuple-element.308, ...), kind=kOutput, calls=%fused_computation.10.clone.1 | convolution fusion | flops 411107328 | bytes 8532481 | tf_op jit(solution)/shard_map/while/body/eval_jaxpr/hgqk,khd->hgqd/dot_general | solution.py:74
  150.9 1.6 fusion.68
  152.5 0.6 dynamic_slice.38
  154.3 4.8 %fusion.66 = (f32[4,384]{1,0:T(4,128)S(1)}, f32[1024,384,4]{1,0,2:T(8,128)}) fusion(pred[384,1024]{0,1:T(8,128)(4,1)S(1)} %broadcast_compare_fusion.2, bf16[384,1,4,128]{3,0,2,1:T(8,128)(2,1)S(1)} %get-tuple-element.342, bf16[12,1024,1,128]{3,1,2,0:T(8,128)(2,1)} %get-tuple-element.341, s32[]{:T(128)} %get-tuple-element.322), kind=kOutput, calls=%fused_computation.3.clone.1 | convolution fusion | flops 407370240 | bytes 7346688 | tf_op jit(solution)/shard_map/while/body/eval_jaxpr/qhgd,khd->hgqk/dot_general | solution.py:66
  159.1 4.8 %fusion.69 = f32[1,4,384,128]{3,2,1,0:T(8,128)S(1)} fusion(f32[1024,384,4]{1,0,2:T(8,128)} %get-tuple-element.307, f32[4,384]{1,0:T(4,128)S(1)} %bitcast.111, pred[384,1024]{0,1:T(8,128)(4,1)S(1)} %broadcast_compare_fusion.2, f32[1,4,384,128]{3,2,1,0:T(8,128)S(1)} %get-tuple-element.325, f32[4,384]{1,0:T(4,128)S(1)} %get-tuple-element.308, ...), kind=kOutput, calls=%fused_computation.10.clone.1 | convolution fusion | flops 411107328 | bytes 8532481 | tf_op jit(solution)/shard_map/while/body/eval_jaxpr/hgqk,khd->hgqd/dot_general | solution.py:74
  163.9 1.6 fusion.68
  165.5 0.6 dynamic_slice.38
  167.4 4.8 %fusion.66 = (f32[4,384]{1,0:T(4,128)S(1)}, f32[1024,384,4]{1,0,2:T(8,128)}) fusion(pred[384,1024]{0,1:T(8,128)(4,1)S(1)} %broadcast_compare_fusion.2, bf16[384,1,4,128]{3,0,2,1:T(8,128)(2,1)S(1)} %get-tuple-element.342, bf16[12,1024,1,128]{3,1,2,0:T(8,128)(2,1)} %get-tuple-element.341, s32[]{:T(128)} %get-tuple-element.322), kind=kOutput, calls=%fused_computation.3.clone.1 | convolution fusion | flops 407370240 | bytes 7346688 | tf_op jit(solution)/shard_map/while/body/eval_jaxpr/qhgd,khd->hgqk/dot_general | solution.py:66
  172.2 4.8 %fusion.69 = f32[1,4,384,128]{3,2,1,0:T(8,128)S(1)} fusion(f32[1024,384,4]{1,0,2:T(8,128)} %get-tuple-element.307, f32[4,384]{1,0:T(4,128)S(1)} %bitcast.111, pred[384,1024]{0,1:T(8,128)(4,1)S(1)} %broadcast_compare_fusion.2, f32[1,4,384,128]{3,2,1,0:T(8,128)S(1)} %get-tuple-element.325, f32[4,384]{1,0:T(4,128)S(1)} %get-tuple-element.308, ...), kind=kOutput, calls=%fused_computation.10.clone.1 | convolution fusion | flops 411107328 | bytes 8532481 | tf_op jit(solution)/shard_map/while/body/eval_jaxpr/hgqk,khd->hgqd/dot_general | solution.py:74
  177.0 1.6 fusion.68
  178.6 0.6 dynamic_slice.38
  180.4 4.8 %fusion.66 = (f32[4,384]{1,0:T(4,128)S(1)}, f32[1024,384,4]{1,0,2:T(8,128)}) fusion(pred[384,1024]{0,1:T(8,128)(4,1)S(1)} %broadcast_compare_fusion.2, bf16[384,1,4,128]{3,0,2,1:T(8,128)(2,1)S(1)} %get-tuple-element.342, bf16[12,1024,1,128]{3,1,2,0:T(8,128)(2,1)} %get-tuple-element.341, s32[]{:T(128)} %get-tuple-element.322), kind=kOutput, calls=%fused_computation.3.clone.1 | convolution fusion | flops 407370240 | bytes 7346688 | tf_op jit(solution)/shard_map/while/body/eval_jaxpr/qhgd,khd->hgqk/dot_general | solution.py:66
  185.2 4.8 %fusion.69 = f32[1,4,384,128]{3,2,1,0:T(8,128)S(1)} fusion(f32[1024,384,4]{1,0,2:T(8,128)} %get-tuple-element.307, f32[4,384]{1,0:T(4,128)S(1)} %bitcast.111, pred[384,1024]{0,1:T(8,128)(4,1)S(1)} %broadcast_compare_fusion.2, f32[1,4,384,128]{3,2,1,0:T(8,128)S(1)} %get-tuple-element.325, f32[4,384]{1,0:T(4,128)S(1)} %get-tuple-element.308, ...), kind=kOutput, calls=%fused_computation.10.clone.1 | convolution fusion | flops 411107328 | bytes 8532481 | tf_op jit(solution)/shard_map/while/body/eval_jaxpr/hgqk,khd->hgqd/dot_general | solution.py:74
  190.0 1.6 fusion.68
  191.6 0.6 dynamic_slice.38
  193.5 4.8 %fusion.66 = (f32[4,384]{1,0:T(4,128)S(1)}, f32[1024,384,4]{1,0,2:T(8,128)}) fusion(pred[384,1024]{0,1:T(8,128)(4,1)S(1)} %broadcast_compare_fusion.2, bf16[384,1,4,128]{3,0,2,1:T(8,128)(2,1)S(1)} %get-tuple-element.342, bf16[12,1024,1,128]{3,1,2,0:T(8,128)(2,1)} %get-tuple-element.341, s32[]{:T(128)} %get-tuple-element.322), kind=kOutput, calls=%fused_computation.3.clone.1 | convolution fusion | flops 407370240 | bytes 7346688 | tf_op jit(solution)/shard_map/while/body/eval_jaxpr/qhgd,khd->hgqk/dot_general | solution.py:66
  198.3 4.8 %fusion.69 = f32[1,4,384,128]{3,2,1,0:T(8,128)S(1)} fusion(f32[1024,384,4]{1,0,2:T(8,128)} %get-tuple-element.307, f32[4,384]{1,0:T(4,128)S(1)} %bitcast.111, pred[384,1024]{0,1:T(8,128)(4,1)S(1)} %broadcast_compare_fusion.2, f32[1,4,384,128]{3,2,1,0:T(8,128)S(1)} %get-tuple-element.325, f32[4,384]{1,0:T(4,128)S(1)} %get-tuple-element.308, ...), kind=kOutput, calls=%fused_computation.10.clone.1 | convolution fusion | flops 411107328 | bytes 8532481 | tf_op jit(solution)/shard_map/while/body/eval_jaxpr/hgqk,khd->hgqd/dot_general | solution.py:74
  203.1 1.6 fusion.68
  204.7 0.6 dynamic_slice.38
  206.5 4.8 %fusion.66 = (f32[4,384]{1,0:T(4,128)S(1)}, f32[1024,384,4]{1,0,2:T(8,128)}) fusion(pred[384,1024]{0,1:T(8,128)(4,1)S(1)} %broadcast_compare_fusion.2, bf16[384,1,4,128]{3,0,2,1:T(8,128)(2,1)S(1)} %get-tuple-element.342, bf16[12,1024,1,128]{3,1,2,0:T(8,128)(2,1)} %get-tuple-element.341, s32[]{:T(128)} %get-tuple-element.322), kind=kOutput, calls=%fused_computation.3.clone.1 | convolution fusion | flops 407370240 | bytes 7346688 | tf_op jit(solution)/shard_map/while/body/eval_jaxpr/qhgd,khd->hgqk/dot_general | solution.py:66
  211.3 4.8 %fusion.69 = f32[1,4,384,128]{3,2,1,0:T(8,128)S(1)} fusion(f32[1024,384,4]{1,0,2:T(8,128)} %get-tuple-element.307, f32[4,384]{1,0:T(4,128)S(1)} %bitcast.111, pred[384,1024]{0,1:T(8,128)(4,1)S(1)} %broadcast_compare_fusion.2, f32[1,4,384,128]{3,2,1,0:T(8,128)S(1)} %get-tuple-element.325, f32[4,384]{1,0:T(4,128)S(1)} %get-tuple-element.308, ...), kind=kOutput, calls=%fused_computation.10.clone.1 | convolution fusion | flops 411107328 | bytes 8532481 | tf_op jit(solution)/shard_map/while/body/eval_jaxpr/hgqk,khd->hgqd/dot_general | solution.py:74
  216.1 1.6 fusion.68
  217.7 0.6 dynamic_slice.38
  219.6 4.8 %fusion.66 = (f32[4,384]{1,0:T(4,128)S(1)}, f32[1024,384,4]{1,0,2:T(8,128)}) fusion(pred[384,1024]{0,1:T(8,128)(4,1)S(1)} %broadcast_compare_fusion.2, bf16[384,1,4,128]{3,0,2,1:T(8,128)(2,1)S(1)} %get-tuple-element.342, bf16[12,1024,1,128]{3,1,2,0:T(8,128)(2,1)} %get-tuple-element.341, s32[]{:T(128)} %get-tuple-element.322), kind=kOutput, calls=%fused_computation.3.clone.1 | convolution fusion | flops 407370240 | bytes 7346688 | tf_op jit(solution)/shard_map/while/body/eval_jaxpr/qhgd,khd->hgqk/dot_general | solution.py:66
  224.4 4.8 %fusion.69 = f32[1,4,384,128]{3,2,1,0:T(8,128)S(1)} fusion(f32[1024,384,4]{1,0,2:T(8,128)} %get-tuple-element.307, f32[4,384]{1,0:T(4,128)S(1)} %bitcast.111, pred[384,1024]{0,1:T(8,128)(4,1)S(1)} %broadcast_compare_fusion.2, f32[1,4,384,128]{3,2,1,0:T(8,128)S(1)} %get-tuple-element.325, f32[4,384]{1,0:T(4,128)S(1)} %get-tuple-element.308, ...), kind=kOutput, calls=%fused_computation.10.clone.1 | convolution fusion | flops 411107328 | bytes 8532481 | tf_op jit(solution)/shard_map/while/body/eval_jaxpr/hgqk,khd->hgqd/dot_general | solution.py:74
  229.2 1.6 fusion.68
  230.8 0.6 dynamic_slice.38
  232.6 4.8 %fusion.66 = (f32[4,384]{1,0:T(4,128)S(1)}, f32[1024,384,4]{1,0,2:T(8,128)}) fusion(pred[384,1024]{0,1:T(8,128)(4,1)S(1)} %broadcast_compare_fusion.2, bf16[384,1,4,128]{3,0,2,1:T(8,128)(2,1)S(1)} %get-tuple-element.342, bf16[12,1024,1,128]{3,1,2,0:T(8,128)(2,1)} %get-tuple-element.341, s32[]{:T(128)} %get-tuple-element.322), kind=kOutput, calls=%fused_computation.3.clone.1 | convolution fusion | flops 407370240 | bytes 7346688 | tf_op jit(solution)/shard_map/while/body/eval_jaxpr/qhgd,khd->hgqk/dot_general | solution.py:66
  237.4 4.8 %fusion.69 = f32[1,4,384,128]{3,2,1,0:T(8,128)S(1)} fusion(f32[1024,384,4]{1,0,2:T(8,128)} %get-tuple-element.307, f32[4,384]{1,0:T(4,128)S(1)} %bitcast.111, pred[384,1024]{0,1:T(8,128)(4,1)S(1)} %broadcast_compare_fusion.2, f32[1,4,384,128]{3,2,1,0:T(8,128)S(1)} %get-tuple-element.325, f32[4,384]{1,0:T(4,128)S(1)} %get-tuple-element.308, ...), kind=kOutput, calls=%fused_computation.10.clone.1 | convolution fusion | flops 411107328 | bytes 8532481 | tf_op jit(solution)/shard_map/while/body/eval_jaxpr/hgqk,khd->hgqd/dot_general | solution.py:74
  242.3 1.6 fusion.68
  244.2 4.0 %convolution_convert_fusion = bf16[384,4096]{1,0:T(8,128)(2,1)S(1)} fusion(bf16[384,512]{0,1:T(8,128)(2,1)S(1)} %bitcast.114, bf16[512,4096]{1,0:T(8,128)(2,1)} %param.14), kind=kOutput, calls=%fused_computation.44 | convolution fusion | flops 1612185600 | bytes 7733248 | tf_op jit(solution)/shard_map/dot_general | solution.py:107
  248.5 44.2 %all_to_all.5 = bf16[8,384,512]{2,1,0:T(8,128)(2,1)S(1)} all-to-all(bf16[8,384,512]{2,1,0:T(8,128)(2,1)S(1)} %bitcast.104), channel_id=1, replica_groups=mesh['ctx'=32,'head'=8] {'head'}, dimensions={0} | all-to-all | bytes 6291456 | tf_op jit(solution)/shard_map/all_to_all | solution.py:26
  292.7 0.7 reduce_sum.55
  293.4 0.8 slice.4
  294.2 1.7 rev.4
  296.0 0.4 copy.49
  296.5 67.8 %all-gather.5.cloned.1.call-done = bf16[64,127,512]{2,1,0:T(8,128)(2,1)} async-done(((bf16[2,127,512]{2,1,0:T(8,128)(2,1)}), bf16[64,127,512]{2,1,0:T(8,128)(2,1)}) %all-gather.5.cloned.1.call-update) | async-done | bytes 8323088 | tf_op jit(solution)/shard_map/all_gather | solution.py:114
  364.3 12.2 %fusion.35 = bf16[2,127,512]{2,0,1:T(2,128)(2,1)S(1)} fusion(bf16[64,127,512]{2,1,0:T(8,128)(2,1)} %all-gather.5.cloned.1.call-done, s32[64]{0:T(128)S(1)} %select_reduce_fusion.1, s32[2]{0:T(128)S(1)} %get-tuple-element.238), kind=kOutput, calls=%fused_computation.46 | convolution fusion | flops 16776320 | bytes 8583432 | tf_op jit(solution)/shard_map/sn,nrc->src/dot_general | solution.py:118
  376.5 7.5 %fusion.39 = f32[2,192,512]{2,0,1:T(2,128)S(1)} fusion(bf16[2,192,512]{2,0,1:T(2,128)(2,1)S(1)} %copy.49, bf16[2,127,512]{2,0,1:T(2,128)(2,1)S(1)} %fusion.35, f32[128,1,512]{2,0,1:T(8,128)S(1)} %bitcast.116), kind=kOutput, calls=%fused_computation.51 | convolution fusion | flops 303296512 | bytes 1701888 | tf_op jit(solution)/shard_map/conv_general_dilated | solution.py:124
  384.1 0.9 fusion.38
  (153 shorter events, 8.3 us)
Async XLA Ops:
  6.5 75.9 %all-gather.3.cloned.1.call-start = ((), (), s32[]{:S(2)}) async-start(), calls=%async_computation.1 | async-start | bytes 6488064 | tf_op jit(solution)/shard_map/all_gather | solution.py:14
  8.2 356.1 %all-gather.5.cloned.1.call-start = ((), (), s32[]{:S(2)}) async-start(), calls=%async_computation.2 | async-start | bytes 8650752 | tf_op jit(solution)/shard_map/all_gather | solution.py:114
  10.6 76.6 %copy-start.2 = (s32[64]{0:T(128)S(1)}, s32[64]{0:T(128)}, u32[]{:S(2)}) copy-start(s32[64]{0:T(128)} %param.10) | copy-start | bytes 772
  93.8 4.8 %copy-start = (f32[1024,384,4]{1,0,2:T(8,128)S(1)}, f32[1024,384,4]{1,0,2:T(8,128)}, u32[]{:S(2)}) copy-start(f32[1024,384,4]{1,0,2:T(8,128)} %get-tuple-element.307) | copy-start | bytes 18874372 | tf_op jit(solution)/shard_map/while
  106.9 4.8 %copy-start = (f32[1024,384,4]{1,0,2:T(8,128)S(1)}, f32[1024,384,4]{1,0,2:T(8,128)}, u32[]{:S(2)}) copy-start(f32[1024,384,4]{1,0,2:T(8,128)} %get-tuple-element.307) | copy-start | bytes 18874372 | tf_op jit(solution)/shard_map/while
  119.9 4.8 %copy-start = (f32[1024,384,4]{1,0,2:T(8,128)S(1)}, f32[1024,384,4]{1,0,2:T(8,128)}, u32[]{:S(2)}) copy-start(f32[1024,384,4]{1,0,2:T(8,128)} %get-tuple-element.307) | copy-start | bytes 18874372 | tf_op jit(solution)/shard_map/while
  133.0 4.8 %copy-start = (f32[1024,384,4]{1,0,2:T(8,128)S(1)}, f32[1024,384,4]{1,0,2:T(8,128)}, u32[]{:S(2)}) copy-start(f32[1024,384,4]{1,0,2:T(8,128)} %get-tuple-element.307) | copy-start | bytes 18874372 | tf_op jit(solution)/shard_map/while
  146.0 4.8 %copy-start = (f32[1024,384,4]{1,0,2:T(8,128)S(1)}, f32[1024,384,4]{1,0,2:T(8,128)}, u32[]{:S(2)}) copy-start(f32[1024,384,4]{1,0,2:T(8,128)} %get-tuple-element.307) | copy-start | bytes 18874372 | tf_op jit(solution)/shard_map/while
  159.1 4.8 %copy-start = (f32[1024,384,4]{1,0,2:T(8,128)S(1)}, f32[1024,384,4]{1,0,2:T(8,128)}, u32[]{:S(2)}) copy-start(f32[1024,384,4]{1,0,2:T(8,128)} %get-tuple-element.307) | copy-start | bytes 18874372 | tf_op jit(solution)/shard_map/while
  172.2 4.8 %copy-start = (f32[1024,384,4]{1,0,2:T(8,128)S(1)}, f32[1024,384,4]{1,0,2:T(8,128)}, u32[]{:S(2)}) copy-start(f32[1024,384,4]{1,0,2:T(8,128)} %get-tuple-element.307) | copy-start | bytes 18874372 | tf_op jit(solution)/shard_map/while
  185.2 4.8 %copy-start = (f32[1024,384,4]{1,0,2:T(8,128)S(1)}, f32[1024,384,4]{1,0,2:T(8,128)}, u32[]{:S(2)}) copy-start(f32[1024,384,4]{1,0,2:T(8,128)} %get-tuple-element.307) | copy-start | bytes 18874372 | tf_op jit(solution)/shard_map/while
  198.3 4.8 %copy-start = (f32[1024,384,4]{1,0,2:T(8,128)S(1)}, f32[1024,384,4]{1,0,2:T(8,128)}, u32[]{:S(2)}) copy-start(f32[1024,384,4]{1,0,2:T(8,128)} %get-tuple-element.307) | copy-start | bytes 18874372 | tf_op jit(solution)/shard_map/while
  211.3 4.8 %copy-start = (f32[1024,384,4]{1,0,2:T(8,128)S(1)}, f32[1024,384,4]{1,0,2:T(8,128)}, u32[]{:S(2)}) copy-start(f32[1024,384,4]{1,0,2:T(8,128)} %get-tuple-element.307) | copy-start | bytes 18874372 | tf_op jit(solution)/shard_map/while
  224.4 4.8 %copy-start = (f32[1024,384,4]{1,0,2:T(8,128)S(1)}, f32[1024,384,4]{1,0,2:T(8,128)}, u32[]{:S(2)}) copy-start(f32[1024,384,4]{1,0,2:T(8,128)} %get-tuple-element.307) | copy-start | bytes 18874372 | tf_op jit(solution)/shard_map/while
  237.4 4.8 %copy-start = (f32[1024,384,4]{1,0,2:T(8,128)S(1)}, f32[1024,384,4]{1,0,2:T(8,128)}, u32[]{:S(2)}) copy-start(f32[1024,384,4]{1,0,2:T(8,128)} %get-tuple-element.307) | copy-start | bytes 18874372 | tf_op jit(solution)/shard_map/while
  376.5 7.5 %copy-start.1 = (bf16[384,512]{1,0:T(8,128)(2,1)S(1)}, bf16[384,512]{1,0:T(8,128)(2,1)}, u32[]{:S(2)}) copy-start(bf16[384,512]{1,0:T(8,128)(2,1)} %param.17) | copy-start | bytes 1179652
  376.5 7.5 %copy-start.3 = (f32[512]{0:T(512)S(1)}, f32[512]{0:T(512)}, u32[]{:S(2)}) copy-start(f32[512]{0:T(512)} %param.16) | copy-start | bytes 6148
Sparse Core Ops, SparseCore 0:
  9.2 73.2 all-gather.2
  294.3 69.9 all-gather.4
where the time goes:
time: 393 us; the launch traced here: 392 us
  waiting for transfers between devices  140 us (36%)
  matrix products  139 us (35%)
  blocking collectives  44.2 us (11%)
  other arithmetic  29.1 us (7%)
  local copies, waits for them, and re-layouts  17.8 us (5%)
  between operations  13.5 us (3%)
  loops' own time  8.67 us (2%)
    all_gather x1, waiting for transfers between devices, side_by_side(): out = lax.all_gather(both, axis, axis=dim, tiled=True)  71.8 us
    all_gather x1, waiting for transfers between devices, shards(): piece = lax.all_gather(tail_rows, 'ctx', axis=0, tiled=True)  67.8 us
    dot_general x12, matrix products, attend_block(): jnp.einsum('hgqk,khd->hgqd', weight.astype(jnp.bfloat16), value_block, pr...  57.8 us
    dot_general x12, matrix products, attend_block(): jnp.einsum('qhgd,khd->hgqk', query_heads, key_block, preferred_element_ty...  57.3 us
    all_to_all x1, blocking collectives, sum_at_owner(): tiles = lax.all_to_all(in_blocks(x, dim, size), axis, 0, 0, tiled=True)  44.2 us
    reduce_sum x12, other arithmetic, attend_block(): row_total = row_total * factor + jnp.sum(weight, axis=-1)  18.6 us
    dot_general x1, matrix products, shards(): jnp.einsum('sn,nrc->src', matches, piece, preferred_element_type=jnp.floa...  12.2 us
    another operation x1, loops' own time, shards(): lax.scan(one_step, start_state, (key_split, value_split, jnp.arange(steps...  8.67 us
  transfers between devices with their start and end apart: 2, of which 2 were waited for; matrix products, arithmetic and copies ran while one was open for 1% of the time, Pallas kernels for 0%

commit v1 on v0

--- a/solution.py
+++ b/solution.py
@@ -6,6 +6,13 @@
 
 HEAD_WIDTH = 128
 QUERY_PER_KV = 4
+
+
+def all_by_exchange(shard, mesh_axis, dim):
+    size = lax.axis_size(mesh_axis)
+    shards = jnp.stack([shard for _ in range(size)])
+    shards = lax.all_to_all(shards, mesh_axis, split_axis=0, concat_axis=0)
+    return jnp.concatenate(shards, axis=dim)
 
 
 def side_by_side(arrays, axis, dim, along):
@@ -111,7 +118,7 @@
     blocks_here = projected.reshape(2, block_rows, channels)
     tail_rows = blocks_here[:, block_rows - reach_rows :, :]
     wanted = own_order - 1
-    piece = lax.all_gather(tail_rows, "ctx", axis=0, tiled=True)
+    piece = all_by_exchange(tail_rows, "ctx", 0)
     piece_count = piece.shape[0]
     held_blocks = lookup(block_order, jnp.arange(piece_count, dtype=jnp.int32))
     matches = (held_blocks[None, :] == wanted[:, None]).astype(jnp.bfloat16)

time: 393 us -> 540 us (1.37)
  waiting for transfers between devices: 140 us -> 256 us
  local copies, waits for them, and re-layouts: 17.8 us -> 47.2 us
  starting transfers between devices: 0.04 us -> 8.44 us
  matrix products: 139 us -> 131 us
    all_to_all x0 -> x1, waiting for transfers between devices: none -> 184 us  [all_by_exchange(): shards = lax.all_to_all(shards, mesh_axis, split_axis=0, concat_axis=0)]
    all_gather x1 -> x0, waiting for transfers between devices: 67.8 us -> none  [shards(): piece = lax.all_gather(tail_rows, 'ctx', axis=0, tiled=True)]
    reshape x0 -> x1, local copies, waits for them, and re-layouts: none -> 17.8 us  [all_by_exchange(): return jnp.concatenate(shards, axis=dim)]
    all_to_all x0 -> x1, starting transfers between devices: none -> 8.44 us  [all_by_exchange(): shards = lax.all_to_all(shards, mesh_axis, split_axis=0, concat_axis=0)]
    all_to_all x0 -> x1, local copies, waits for them, and re-layouts: none -> 8.05 us  [all_by_exchange(): shards = lax.all_to_all(shards, mesh_axis, split_axis=0, concat_axis=0)]
    dot_general x1, matrix products: 12.2 us -> 4.6 us  [shards(): jnp.einsum('sn,nrc->src', matches, piece, preferred_element_type=jnp.floa...]
    another operation x0 -> x1, local copies, waits for them, and re-layouts: none -> 5.64 us  [all_by_exchange(): shards = jnp.stack([shard for _ in range(size)])]
where the time goes in v1:
time: 540 us; the launch traced here: 539 us
  waiting for transfers between devices  256 us (47%)
  matrix products  131 us (24%)
  local copies, waits for them, and re-layouts  47.2 us (9%)
  blocking collectives  44.3 us (8%)
  other arithmetic  29.1 us (5%)
  between operations  13.6 us (3%)
  loops' own time  8.67 us (2%)
  starting transfers between devices  8.44 us (2%)
    all_to_all x1, waiting for transfers between devices, all_by_exchange(): shards = lax.all_to_all(shards, mesh_axis, split_axis=0, concat_axis=0)  184 us
    all_gather x1, waiting for transfers between devices, side_by_side(): out = lax.all_gather(both, axis, axis=dim, tiled=True)  71.9 us
    dot_general x12, matrix products, attend_block(): jnp.einsum('hgqk,khd->hgqd', weight.astype(jnp.bfloat16), value_block, pr...  57.8 us
    dot_general x12, matrix products, attend_block(): jnp.einsum('qhgd,khd->hgqk', query_heads, key_block, preferred_element_ty...  57.3 us
    all_to_all x1, blocking collectives, sum_at_owner(): tiles = lax.all_to_all(in_blocks(x, dim, size), axis, 0, 0, tiled=True)  44.3 us
    reduce_sum x12, other arithmetic, attend_block(): row_total = row_total * factor + jnp.sum(weight, axis=-1)  18.6 us
    reshape x1, local copies, waits for them, and re-layouts, all_by_exchange(): return jnp.concatenate(shards, axis=dim)  17.8 us
  transfers between devices with their start and end apart: 2, of which 2 were waited for; matrix products, arithmetic and copies ran while one was open for 1% of the time, Pallas kernels for 0%

profile of v1, /device:TPU:1, one launch (start us, length us, event | category | flops | bytes accessed | tf_op | source)
XLA Modules:
  0.0 538.8 jit_solution(17708577920533310635)
XLA Ops:
  6.5 1.6 pad_maximum_fusion
  8.2 1.2 copy.46
  9.7 0.8 fusion.41
  10.6 71.9 %all-gather.2.cloned.1.call-done = bf16[12288,256]{1,0:T(8,128)(2,1)} async-done(((bf16[384,256]{1,0:T(8,128)(2,1)}), bf16[12288,256]{1,0:T(8,128)(2,1)}) %all-gather.2.cloned.1.call-update) | async-done | bytes 6291472 | tf_op jit(solution)/shard_map/all_gather | solution.py:21
  82.5 4.7 fusion.45
  87.2 156.6 %while.17 = (s32[]{:T(128)}, f32[1,4,384]{2,1,0:T(4,128)S(1)}, f32[1,4,384]{2,1,0:T(4,128)S(1)}, f32[1,4,384,128]{3,2,1,0:T(8,128)S(1)}, s32[12]{0:T(128)S(1)}, ...) while((s32[]{:T(128)}, f32[1,4,384]{2,1,0:T(4,128)S(1)}, ...), condition=%wide.region_6.7_spmd.clone, body=%wide.region_2.6_spmd.clone.sunk | while | flops 826960256 | bytes 48233928 | solution.py:105
  87.2 0.6 dynamic_slice.38
  89.1 4.8 fusion.62
  93.9 4.8 fusion.65
  98.7 1.6 fusion.64
  100.3 0.6 dynamic_slice.38
  102.1 4.8 fusion.62
  106.9 4.8 fusion.65
  111.7 1.6 fusion.64
  113.3 0.6 dynamic_slice.38
  115.2 4.8 fusion.62
  120.0 4.8 fusion.65
  124.8 1.6 fusion.64
  126.4 0.6 dynamic_slice.38
  128.2 4.8 fusion.62
  133.0 4.8 fusion.65
  137.9 1.6 fusion.64
  139.4 0.6 dynamic_slice.38
  141.3 4.8 fusion.62
  146.1 4.8 fusion.65
  150.9 1.6 fusion.64
  152.5 0.6 dynamic_slice.38
  154.3 4.8 fusion.62
  159.1 4.8 fusion.65
  164.0 1.6 fusion.64
  165.6 0.6 dynamic_slice.38
  167.4 4.8 fusion.62
  172.2 4.8 fusion.65
  177.0 1.6 fusion.64
  178.6 0.6 dynamic_slice.38
  180.4 4.8 fusion.62
  185.2 4.8 fusion.65
  190.1 1.6 fusion.64
  191.7 0.6 dynamic_slice.38
  193.5 4.8 fusion.62
  198.3 4.8 fusion.65
  203.1 1.6 fusion.64
  206.5 4.8 fusion.62
  211.3 4.8 fusion.65
  216.2 1.6 fusion.64
  217.8 0.6 dynamic_slice.38
  219.6 4.8 fusion.62
  224.4 4.8 fusion.65
  229.2 1.6 fusion.64
  230.8 0.6 dynamic_slice.38
  232.6 4.8 fusion.62
  237.4 4.8 fusion.65
  242.3 1.6 fusion.64
  244.2 4.0 convolution_convert_fusion
  248.5 44.3 %all_to_all.10 = bf16[8,384,512]{2,1,0:T(8,128)(2,1)S(1)} all-to-all(bf16[8,384,512]{2,1,0:T(8,128)(2,1)S(1)} %bitcast.107), channel_id=1, replica_groups=mesh['ctx'=32,'head'=8] {'head'}, dimensions={0} | all-to-all | bytes 6291456 | tf_op jit(solution)/shard_map/all_to_all | solution.py:33
  292.9 0.7 reduce_sum.55
  293.9 5.6 %stack.2 = bf16[32,2,127,512]{3,1,2,0:T(2,128)(2,1)} broadcast(bf16[2,127,512]{2,0,1:T(2,128)(2,1)S(1)} %copy.50), dimensions={1,2,3} | broadcast | bytes 8583168 | tf_op jit(solution)/shard_map/stack | solution.py:13
  299.5 8.4 %all-to-all-start.1 = ((bf16[32,2,127,512]{3,1,2,0:T(2,128)(2,1)}), bf16[32,2,127,512]{3,1,2,0:T(2,128)(2,1)}, u32[]{:S(2)}, u32[]{:S(2)}) async-start(bf16[32,2,127,512]{3,1,2,0:T(2,128)(2,1)} %stack.2), calls=%async_computation.1 | async-start | bytes 16646144 | tf_op jit(solution)/shard_map/all_to_all | solution.py:14
  308.6 184.4 %all-to-all-done.1 = bf16[32,2,127,512]{3,1,2,0:T(2,128)(2,1)} async-done(((bf16[32,2,127,512]{3,1,2,0:T(2,128)(2,1)}), bf16[32,2,127,512]{3,1,2,0:T(2,128)(2,1)}, u32[]{:S(2)}, u32[]{:S(2)}) %all-to-all-start.1) | async-done | bytes 8323104 | tf_op jit(solution)/shard_map/all_to_all | solution.py:14
  493.0 8.1 %copy.51 = bf16[32,2,127,512]{3,1,0,2:T(2,128)(2,1)} copy(bf16[32,2,127,512]{3,1,2,0:T(2,128)(2,1)} %all-to-all-done.1) | data formatting | bytes 16646144 | tf_op jit(solution)/shard_map/all_to_all | solution.py:14
  501.1 17.8 %reshape.136 = bf16[64,127,512]{2,0,1:T(8,128)(2,1)} reshape(bf16[32,2,127,512]{3,1,0,2:T(2,128)(2,1)} %copy.51) | data formatting | bytes 16646144 | tf_op jit(solution)/shard_map/reshape | solution.py:15
  518.8 4.6 convolution_convert_fusion.1
  523.4 7.5 %fusion.34 = f32[2,192,512]{2,0,1:T(2,128)S(1)} fusion(bf16[2,192,512]{2,0,1:T(2,128)(2,1)S(1)} %copy.52, bf16[2,127,512]{2,0,1:T(2,128)(2,1)S(1)} %convolution_convert_fusion.1, f32[128,1,512]{2,0,1:T(8,128)S(1)} %bitcast.119), kind=kOutput, calls=%fused_computation.49 | convolution fusion | flops 303296512 | bytes 1701888 | tf_op jit(solution)/shard_map/conv_general_dilated | solution.py:131
  531.0 0.9 fusion.33
  (158 shorter events, 9.8 us)
Async XLA Ops:
  6.5 75.9 %all-gather.2.cloned.1.call-start = ((), (), s32[]{:S(2)}) async-start(), calls=%async_computation.2 | async-start | bytes 6488064 | tf_op jit(solution)/shard_map/all_gather | solution.py:21
  10.5 76.7 %copy-start.3 = (s32[64]{0:T(128)S(1)}, s32[64]{0:T(128)}, u32[]{:S(2)}) copy-start(s32[64]{0:T(128)} %param.10) | copy-start | bytes 772
  93.9 4.8 copy-start
  106.9 4.8 copy-start
  120.0 4.8 copy-start
  133.0 4.8 copy-start
  146.1 4.8 copy-start
  159.1 4.8 copy-start
  172.2 4.8 copy-start
  185.2 4.8 copy-start
  198.3 4.8 copy-start
  211.3 4.8 copy-start
  224.4 4.8 copy-start
  237.4 4.8 copy-start
  299.5 8.4 %copy-start.2 = (f32[128,512]{1,0:T(8,128)S(1)}, f32[128,512]{1,0:T(8,128)}, u32[]{:S(2)}) copy-start(f32[128,512]{1,0:T(8,128)} %param.15) | copy-start | bytes 786436
  299.5 193.5 %all-to-all-start.1 = ((bf16[32,2,127,512]{3,1,2,0:T(2,128)(2,1)}), bf16[32,2,127,512]{3,1,2,0:T(2,128)(2,1)}, u32[]{:S(2)}, u32[]{:S(2)}) async-start(bf16[32,2,127,512]{3,1,2,0:T(2,128)(2,1)} %stack.2), calls=%async_computation.1 | async-start | bytes 16646144 | tf_op jit(solution)/shard_map/all_to_all | solution.py:14
  523.4 7.5 %copy-start.1 = (bf16[384,512]{1,0:T(8,128)(2,1)S(1)}, bf16[384,512]{1,0:T(8,128)(2,1)}, u32[]{:S(2)}) copy-start(bf16[384,512]{1,0:T(8,128)(2,1)} %param.17) | copy-start | bytes 1179652
  523.4 7.5 %copy-start.4 = (f32[512]{0:T(512)S(1)}, f32[512]{0:T(512)}, u32[]{:S(2)}) copy-start(f32[512]{0:T(512)} %param.16) | copy-start | bytes 6148
Sparse Core Ops, SparseCore 0:
  9.2 73.2 all-gather.1
